TPU v7x, 128 devices: a whole 4x4x4 slice. The times are simulated.
128 devices in a mesh: seq: 8 (over z, core), tp: 16 (over x, y).
Axes of the slice: x: 4, y: 4, z: 4, core: 2. Of those that a mesh axis runs over, the one named last changes fastest.
Arguments:
- patches: bfloat16 [32768, 1280], P(('seq', 'tp')), may hold values from -6 to 6
- image_table: int32 [256, 3], replicated, may hold values from 0 to 4095, as said below
- ln_gain: float32 [1280], replicated, may hold values from 0.25 to 1.75
- ln_bias: float32 [1280], replicated, may hold values from -3 to 3
- merge_up: bfloat16 [5120, 5120], P(None, 'tp'), may hold values from -0.078125 to 0.078125
- merge_up_bias: float32 [5120], P('tp'), may hold values from -3 to 3
- merge_down: bfloat16 [5120, 3584], P('tp'), may hold values from -0.15625 to 0.15625
- merge_down_bias: float32 [3584], replicated, may hold values from -3 to 3
- text_embeds: bfloat16 [4096, 3584], P('seq', 'tp'), may hold values from -6 to 6
- attn_gain: float32 [3584], replicated, may hold values from 0.25 to 1.75
- q_weight: bfloat16 [3584, 2048], P(None, 'tp'), may hold values from -2 to 2
- q_bias: float32 [2048], P('tp'), may hold values from -3 to 3
- key_value_weight: bfloat16 [3584, 1024], replicated, may hold values from -2 to 2
- key_value_bias: float32 [1024], replicated, may hold values from -3 to 3
- o_weight: bfloat16 [2048, 3584], P('tp'), may hold values from -0.1875 to 0.1875
Outputs:
- block_out: bfloat16 [4096, 3584], P('seq', 'tp')
Inputs may be any that keep to these rules, and one draw needn't show every extreme that they name: `image_table`: grid entries are even. Table rows 2d and 2d + 1 are the two images of device d = seq index * 16 + tp index; the second starts right after the first, so the device's tokens fill consecutive positions inside block [s * 512, (s + 1) * 512) of its seq index s. Images never intersect. The two images of a device hold at most 64 merged tokens, and in every seq group one device holds exactly 64. A sequence block holds at most 424 image tokens, and some block holds exactly that many.
All inputs are finite; a program needn't handle non-finite values.
Results may differ from a plain program's by a relative error of at most 0.012.
Values may be sent and summed in bfloat16 or wider, within the bound.
A program may use at most 128 MiB of HBM per device.

v0:
```python
import jax
import jax.numpy as jnp
from jax import lax
from jax.sharding import PartitionSpec as P

HEAD_DIMENSION = 128
KEY_VALUE_HEADS = 4
LOCAL_QUERY_HEAD = 16
CAP = 64
TOK_SEQ = 512
MW = 5120
EPS = 1e-06
THETA = 1000000.0


def sent_together(arrays, axis, dim, along):
    both = jnp.concatenate(arrays, axis=along)
    out, at, done = (lax.all_gather(both, axis, axis=dim, tiled=True), 0, [])
    for a in arrays:
        done.append(lax.slice_in_dim(out, at, at + a.shape[along], axis=along))
        at += a.shape[along]
    return tuple(done)


def copy_for_each(shard, axis):
    peers = lax.axis_size(axis)
    return lax.all_to_all(
        jnp.broadcast_to(shard[None], (peers, *shard.shape)), axis, 0, 0, tiled=True
    )


def laid_out(pieces, dim):
    lengths = list(pieces.shape[1:])
    lengths[dim] *= pieces.shape[0]
    return jnp.moveaxis(pieces, 0, dim).reshape(lengths)


def gathered_copies(shard, axis, dim):
    pieces = copy_for_each(shard, axis)
    return laid_out(pieces, dim)


def layer_norm(row_data, scale_row, offset_row):
    centre = jnp.mean(row_data, axis=-1, keepdims=True)
    centred = row_data - centre
    spread = jnp.mean(centred * centred, axis=-1, keepdims=True)
    return centred * lax.rsqrt(spread + EPS) * scale_row + offset_row


def image_fields(image_table):
    grid_h = image_table[:, 0]
    grid_w = image_table[:, 1]
    across = grid_w // 2
    return (across, grid_h // 2 * across, image_table[:, 2])


def rope_tables(positions, image_table, head_size):
    across, counts, offsets = image_fields(image_table)
    inside = (
        (positions[:, None] >= offsets[None, :])
        & (positions[:, None] < (offsets + counts)[None, :])
    ).astype(jnp.int32)
    is_image = jnp.sum(inside, axis=1)
    run_start = jnp.sum(inside * offsets[None, :], axis=1)
    row_width = jnp.sum(inside * across[None, :], axis=1) + (1 - is_image)
    inner_index = positions - run_start
    pos_t = jnp.where(is_image > 0, run_start, positions)
    pos_h = jnp.where(is_image > 0, run_start + inner_index // row_width, positions)
    pos_w = jnp.where(is_image > 0, run_start + inner_index % row_width, positions)
    half_size = head_size // 2
    frequency = jnp.arange(half_size, dtype=jnp.int32)
    inverse = THETA ** (-2.0 * frequency.astype(jnp.float32) / head_size)
    first_cut = head_size // 8
    second_cut = first_cut + 3 * head_size // 16
    chosen = jnp.where(
        frequency[None, :] < first_cut,
        pos_t[:, None],
        jnp.where(frequency[None, :] < second_cut, pos_h[:, None], pos_w[:, None]),
    )
    angles = chosen.astype(jnp.float32) * inverse[None, :]
    angles = jnp.concatenate([angles, angles], axis=1)
    return (jnp.cos(angles), jnp.sin(angles), is_image)


def apply_rotation(value_tensor, cosine_values, sine_lookup):
    half_size = value_tensor.shape[-1] // 2
    turned = jnp.concatenate(
        [-value_tensor[..., half_size:], value_tensor[..., :half_size]], axis=-1
    )
    return value_tensor * cosine_values[:, None, :] + turned * sine_lookup[:, None, :]


def merger_hidden(vision, merge_up, merge_up_bias, image_weight):
    lifted = jnp.dot(vision, merge_up, preferred_element_type=jnp.float32) + merge_up_bias
    return (jax.nn.gelu(lifted, approximate=False) * image_weight[:, None]).astype(jnp.bfloat16)


def per_device(
    patches,
    image_table,
    ln_gain,
    ln_bias,
    merge_up,
    merge_up_bias,
    merge_down,
    merge_down_bias,
    text_embeds,
    attn_gain,
    q_weight,
    q_bias,
    key_value_weight,
    key_value_bias,
    o_weight,
):
    tp_count = lax.axis_size("tp")
    seq_index = lax.axis_index("seq")
    tensor_parallel_index = lax.axis_index("tp")
    row_share = TOK_SEQ // tp_count
    column_count = text_embeds.shape[1]
    local_heads = q_weight.shape[1] // HEAD_DIMENSION
    normed = layer_norm(patches.astype(jnp.float32), ln_gain, ln_bias).astype(jnp.bfloat16)
    merged = normed.reshape(CAP, MW)
    block_index = jnp.arange(TOK_SEQ, dtype=jnp.int32)
    positions = seq_index * TOK_SEQ + block_index % row_share * tp_count + block_index // row_share
    cosine_values, sine_lookup, is_image = rope_tables(positions, image_table, HEAD_DIMENSION)
    image_weight = is_image.astype(jnp.float32)
    across, counts, offsets = image_fields(image_table)
    group_begin = 2 * seq_index * tp_count
    group_first = lax.dynamic_slice_in_dim(offsets, group_begin, 2 * tp_count).reshape(tp_count, 2)[
        :, 0
    ]
    group_length = jnp.sum(
        lax.dynamic_slice_in_dim(counts, group_begin, 2 * tp_count).reshape(tp_count, 2), axis=1
    )
    run_start = group_first[tensor_parallel_index]
    run_length = group_length[tensor_parallel_index]
    per_peer = CAP // tp_count + 1
    residue = run_start % tp_count
    slot_index = (
        jnp.arange(tp_count, dtype=jnp.int32)[:, None]
        + jnp.arange(per_peer, dtype=jnp.int32)[None, :] * tp_count
        - residue
    ).reshape(-1)
    live_slot = (slot_index >= 0) & (slot_index < run_length)
    picker = (
        (slot_index[:, None] == jnp.arange(CAP, dtype=jnp.int32)[None, :]) & live_slot[:, None]
    ).astype(jnp.bfloat16)
    outgoing = (
        jnp.dot(picker, merged, preferred_element_type=jnp.float32)
        .astype(jnp.bfloat16)
        .reshape(tp_count, per_peer, MW)
    )
    incoming = lax.all_to_all(outgoing, "tp", split_axis=0, concat_axis=0, tiled=True)
    target = (
        group_first[:, None] // tp_count
        - seq_index * row_share
        + jnp.arange(per_peer, dtype=jnp.int32)[None, :]
    ).reshape(-1)
    placer = (target[None, :] == jnp.arange(row_share, dtype=jnp.int32)[:, None]).astype(
        jnp.bfloat16
    )
    own_rows = jnp.dot(
        placer, incoming.reshape(tp_count * per_peer, MW), preferred_element_type=jnp.float32
    ).astype(jnp.bfloat16)
    weight_rows = image_weight
    hidden = merger_hidden(
        lax.all_gather(own_rows, "tp", axis=0, tiled=True), merge_up, merge_up_bias, weight_rows
    )
    partial_sum = jnp.dot(hidden, merge_down, preferred_element_type=jnp.float32)
    text_rows = (
        text_embeds.reshape(row_share, tp_count, column_count)
        .transpose(1, 0, 2)
        .reshape(TOK_SEQ, column_count)
        .astype(jnp.float32)
    )
    text_rows = text_rows * (1.0 - image_weight)[:, None]
    column_start = tensor_parallel_index * column_count
    single_key_head = tensor_parallel_index * local_heads // (LOCAL_QUERY_HEAD // KEY_VALUE_HEADS)
    key_weight = lax.dynamic_slice_in_dim(
        key_value_weight, single_key_head * HEAD_DIMENSION, HEAD_DIMENSION, 1
    )
    value_matrix = lax.dynamic_slice_in_dim(
        key_value_weight,
        KEY_VALUE_HEADS * HEAD_DIMENSION + single_key_head * HEAD_DIMENSION,
        HEAD_DIMENSION,
        1,
    )
    key_bias = lax.dynamic_slice_in_dim(
        key_value_bias, single_key_head * HEAD_DIMENSION, HEAD_DIMENSION
    )
    bias_of_value = lax.dynamic_slice_in_dim(
        key_value_bias,
        KEY_VALUE_HEADS * HEAD_DIMENSION + single_key_head * HEAD_DIMENSION,
        HEAD_DIMENSION,
    )
    current = lax.dynamic_slice_in_dim(partial_sum, column_start, column_count, 1)
    term = lax.dynamic_update_slice_in_dim(partial_sum, current + text_rows, column_start, 1)
    summed = lax.psum(term, "tp")
    residual = summed + image_weight[:, None] * merge_down_bias[None, :]
    scale_rows = lax.rsqrt(jnp.mean(residual * residual, axis=1) + EPS)
    normed_rows = (residual * scale_rows[:, None] * attn_gain[None, :]).astype(jnp.bfloat16)
    query = jnp.dot(normed_rows, q_weight, preferred_element_type=jnp.float32)
    key_tensor = jnp.dot(normed_rows, key_weight, preferred_element_type=jnp.float32)
    value_tensor = jnp.dot(normed_rows, value_matrix, preferred_element_type=jnp.float32)
    residual_columns = lax.dynamic_slice_in_dim(residual, column_start, column_count, 1)
    query = apply_rotation(
        (query + q_bias).reshape(TOK_SEQ, local_heads, HEAD_DIMENSION), cosine_values, sine_lookup
    ).astype(jnp.bfloat16)
    key_tensor = (
        apply_rotation(
            (key_tensor + key_bias).reshape(TOK_SEQ, 1, HEAD_DIMENSION), cosine_values, sine_lookup
        )
        .reshape(TOK_SEQ, HEAD_DIMENSION)
        .astype(jnp.bfloat16)
    )
    value_tensor = (value_tensor + bias_of_value).astype(jnp.bfloat16)
    score_scale = HEAD_DIMENSION ** (-0.5)
    best_score = jnp.full((local_heads, TOK_SEQ), -1e30, jnp.float32)
    key_piece, value_piece = sent_together((key_tensor, value_tensor), "seq", 0, 1)
    global_row = jnp.arange(key_piece.shape[0], dtype=jnp.int32)
    inner_row = global_row % TOK_SEQ
    key_position = (
        global_row // TOK_SEQ * TOK_SEQ + inner_row % row_share * tp_count + inner_row // row_share
    )
    scores = (
        jnp.einsum("qhd,kd->hqk", query, key_piece, preferred_element_type=jnp.float32)
        * score_scale
    )
    allowed = key_position[None, None, :] <= positions[None, :, None]
    scores = jnp.where(allowed, scores, -1e30)
    fresh_best = jnp.maximum(best_score, jnp.max(scores, axis=2))
    weights = jnp.where(allowed, jnp.exp(scores - fresh_best[:, :, None]), 0.0)
    total_weight = jnp.sum(weights, axis=2)
    accumulated = jnp.einsum(
        "hqk,kd->hqd", weights.astype(jnp.bfloat16), value_piece, preferred_element_type=jnp.float32
    )
    best_score, total_weight, accumulated = (fresh_best, total_weight, accumulated)
    attention = (
        (accumulated / total_weight[:, :, None])
        .astype(jnp.bfloat16)
        .transpose(1, 0, 2)
        .reshape(TOK_SEQ, local_heads * HEAD_DIMENSION)
    )
    weight_cols = lax.all_to_all(o_weight, "tp", split_axis=1, concat_axis=0, tiled=True)
    weight_rows = weight_cols
    mixed = jnp.dot(
        gathered_copies(attention, "tp", 1), weight_rows, preferred_element_type=jnp.float32
    )
    output_rows = residual_columns + mixed
    return (
        output_rows.reshape(tp_count, row_share, column_count)
        .transpose(1, 0, 2)
        .reshape(TOK_SEQ, column_count)
        .astype(jnp.bfloat16)
    )


def solution(mesh):
    return jax.shard_map(
        per_device,
        mesh=mesh,
        in_specs=(
            P(("seq", "tp"), None),
            P(),
            P(),
            P(),
            P(None, "tp"),
            P("tp"),
            P("tp", None),
            P(),
            P("seq", "tp"),
            P(),
            P(None, "tp"),
            P("tp"),
            P(),
            P(),
            P("tp", None),
        ),
        out_specs=P("seq", "tp"),
        check_vma=False,
    )
```

profile of v0, /device:TPU:0, one launch (start us, length us, event | category | flops | bytes accessed | tf_op | source)
XLA Modules:
  0.0 355.0 jit_solution(4391008567551796274)
XLA Ops:
  11.2 1.3 convert_reduce_fusion
  12.5 1.4 fusion.10
  13.9 2.3 fusion.13
  16.2 2.3 reshape.441
  19.1 2.4 convolution_convert_fusion
  21.5 2.3 reshape.442
  23.8 7.2 %all-to-all-start = ((bf16[16,5,5120]{2,1,0:T(8,128)(2,1)}), bf16[16,5,5120]{2,1,0:T(8,128)(2,1)}, u32[]{:S(2)}, u32[]{:S(2)}) async-start(bf16[16,5,5120]{2,1,0:T(8,128)(2,1)} %reshape.442), calls=%async_computation | async-start | bytes 2621440 | tf_op jit(solution)/shard_map/all_to_all | solution.py:153
  31.2 20.6 %all-to-all-done = bf16[16,5,5120]{2,1,0:T(8,128)(2,1)} async-done(((bf16[16,5,5120]{2,1,0:T(8,128)(2,1)}), bf16[16,5,5120]{2,1,0:T(8,128)(2,1)}, u32[]{:S(2)}, u32[]{:S(2)}) %all-to-all-start) | async-done | bytes 819232 | tf_op jit(solution)/shard_map/all_to_all | solution.py:153
  51.9 2.2 reshape.443
  54.1 2.1 convolution_convert_fusion.1
  56.2 1.1 copy.26
  57.4 1.1 copy.27
  59.1 52.2 %all-gather.3.cloned.1.call-done = bf16[512,5120]{1,0:T(8,128)(2,1)} async-done(((bf16[32,5120]{1,0:T(8,128)(2,1)}), bf16[512,5120]{1,0:T(8,128)(2,1)}) %all-gather.3.cloned.1.call-update) | async-done | bytes 5242896 | tf_op jit(solution)/shard_map/all_gather | solution.py:167
  111.3 11.4 %fusion.47 = f32[512,3584]{1,0:T(8,128)} fusion(bf16[320,3584]{1,0:T(8,128)(2,1)} %param.21, bf16[512,5120]{1,0:T(8,128)(2,1)} %all-gather.3.cloned.1.call-done, bf16[5120,320]{0,1:T(8,128)(2,1)S(1)} %copy-done, f32[512]{0:T(512)S(1)} %get-tuple-element.28, f32[320]{0:T(512)S(1)} %copy-done.10), kind=kOutput, calls=%fused_computation.58 | convolution fusion | flops 2863104000 | bytes 18156800 | tf_op jit(solution)/shard_map/dot_general | solution.py:169
  122.7 1.6 fusion.48
  124.3 3.5 dynamic_update_slice.3
  129.1 130.4 %all-reduce.2.cloned.1.call-done = f32[512,3584]{1,0:T(8,128)} async-done(((f32[512,3584]{1,0:T(8,128)}), f32[512,3584]{1,0:T(8,128)}) %all-reduce.2.cloned.1.call-update) | async-done | bytes 7340048 | tf_op jit(solution)/shard_map/psum | solution.py:198
  259.5 4.2 %multiply_reduce_fusion = (f32[512]{0:T(512)S(1)}, f32[512,3584]{1,0:T(8,128)S(1)}) fusion(f32[512,3584]{1,0:T(8,128)} %all-reduce.2.cloned.1.call-done, f32[3584]{0:T(1024)S(1)} %copy-done.6, f32[512]{0:T(512)S(1)} %get-tuple-element.28), kind=kLoop, calls=%fused_computation.3 | loop fusion | flops 7339520 | bytes 14698496 | tf_op jit(solution)/shard_map/reduce_sum | solution.py:200
  263.8 1.1 multiply_convert_fusion
  264.8 1.8 copy-done.3
  266.7 3.2 convolution_add_fusion.3
  270.0 2.6 fusion.23
  272.6 1.0 fusion.88
  274.4 1.3 copy.28
  275.7 5.4 %all-to-all-start.2 = ((bf16[128,16,224]{0,2,1:T(8,128)(2,1)}), bf16[128,16,224]{0,2,1:T(8,128)(2,1)}, u32[]{:S(2)}, u32[]{:S(2)}) async-start(bf16[128,16,224]{0,2,1:T(8,128)(2,1)} %bitcast.18), calls=%async_computation.2 | async-start | bytes 1835008 | tf_op jit(solution)/shard_map/all_to_all | solution.py:244
  281.2 3.4 convolution_add_fusion.1
  284.6 15.3 %all-gather.5.cloned.1.call-done = bf16[4096,256]{0,1:T(8,128)(2,1)} async-done(((bf16[512,256]{0,1:T(8,128)(2,1)}), bf16[4096,256]{0,1:T(8,128)(2,1)}) %all-gather.5.cloned.1.call-update) | async-done | bytes 2097168 | tf_op jit(solution)/shard_map/all_gather | solution.py:18
  299.9 3.8 %fusion = (f32[512]{0:T(512)S(1)}, f32[4096,512]{1,0:T(8,128)S(1)}) fusion(s32[512]{0:T(512)S(1)} %fusion.123, s32[4096]{0:T(1024)S(1)} %fusion.106, f32[512,64]{0,1:T(8,128)S(1)} %convert_multiply_fusion, f32[512,128]{0,1:T(8,128)S(1)} %convolution_add_fusion.1, f32[512,64]{0,1:T(8,128)S(1)} %get-tuple-element.16, f32[512,64]{0,1:T(8,128)S(1)} %get-tuple-element.15, ...), kind=kOutput, calls=%fused_computation.5 | convolution fusion | flops 545652224 | bytes 10113024 | tf_op jit(solution)/shard_map/qhd,kd->hqk/dot_general | solution.py:226
  303.7 2.9 fusion.1
  306.6 3.0 fusion.27
  310.0 35.3 %all_to_all.26 = bf16[16,512,128]{2,1,0:T(8,128)(2,1)S(1)} all-to-all(bf16[16,512,128]{2,1,0:T(8,128)(2,1)S(1)} %broadcast_in_dim.60), channel_id=1, replica_groups=mesh['seq'=8,'tp'=16] {'tp'}, dimensions={0} | all-to-all | bytes 4194304 | tf_op jit(solution)/shard_map/all_to_all | solution.py:27
  345.4 2.1 fusion.20
  (65 shorter events, 7.6 us)
Async XLA Ops:
  6.5 104.8 %copy-start = (bf16[5120,320]{0,1:T(8,128)(2,1)S(1)}, bf16[5120,320]{0,1:T(8,128)(2,1)}, u32[]{:S(2)}) copy-start(bf16[5120,320]{0,1:T(8,128)(2,1)} %param.19) | copy-start | bytes 9830404
  21.5 89.8 %copy-start.10 = (f32[320]{0:T(512)S(1)}, f32[320]{0:T(512)}, u32[]{:S(2)}) copy-start(f32[320]{0:T(512)} %param.20) | copy-start | bytes 3844
  23.8 28.1 %all-to-all-start = ((bf16[16,5,5120]{2,1,0:T(8,128)(2,1)}), bf16[16,5,5120]{2,1,0:T(8,128)(2,1)}, u32[]{:S(2)}, u32[]{:S(2)}) async-start(bf16[16,5,5120]{2,1,0:T(8,128)(2,1)} %reshape.442), calls=%async_computation | async-start | bytes 2621440 | tf_op jit(solution)/shard_map/all_to_all | solution.py:153
  31.0 80.3 %all-gather.3.cloned.1.call-start = ((), (), s32[]{:S(2)}) async-start(), calls=%async_computation.3 | async-start | bytes 5570560 | tf_op jit(solution)/shard_map/all_gather | solution.py:167
  56.2 203.3 %all-reduce.2.cloned.1.call-start = ((), (), s32[]{:S(2)}) async-start(), calls=%async_computation.4 | async-start | bytes 14680064 | tf_op jit(solution)/shard_map/psum | solution.py:198
  122.7 136.8 %copy-start.6 = (f32[3584]{0:T(1024)S(1)}, f32[3584]{0:T(1024)}, u32[]{:S(2)}) copy-start(f32[3584]{0:T(1024)} %param.22) | copy-start | bytes 43012
  127.8 172.1 %all-gather.5.cloned.1.call-start = ((), (), s32[]{:S(2)}) async-start(), calls=%async_computation.5 | async-start | bytes 2359296 | tf_op jit(solution)/shard_map/all_gather | solution.py:18
  129.0 134.7 %copy-start.7 = (f32[3584]{0:T(1024)S(1)}, f32[3584]{0:T(1024)}, u32[]{:S(2)}) copy-start(f32[3584]{0:T(1024)} %param.24) | copy-start | bytes 43012
  263.7 3.0 copy-start.3
  266.7 5.9 %copy-start.2 = (bf16[512,3584]{1,0:T(8,128)(2,1)}, bf16[512,3584]{1,0:T(8,128)(2,1)S(1)}, u32[]{:S(2)}) copy-start(bf16[512,3584]{1,0:T(8,128)(2,1)S(1)} %multiply_convert_fusion) | copy-start | bytes 11010052
  269.9 4.5 %copy-start.4 = (bf16[128,3584]{1,0:T(8,128)(2,1)S(1)}, bf16[128,3584]{1,0:T(8,128)(2,1)}, u32[]{:S(2)}) copy-start(bf16[128,3584]{1,0:T(8,128)(2,1)} %param.29) | copy-start | bytes 2752516
  269.9 11.2 %copy-start.5 = (bf16[3584,128]{1,0:T(8,128)(2,1)S(1)}, bf16[3584,128]{1,0:T(8,128)(2,1)}, u32[]{:S(2)}) copy-start(bf16[3584,128]{1,0:T(8,128)(2,1)} %param.25) | copy-start | bytes 2752516
  270.0 11.2 %copy-start.8 = (f32[128]{0:T(128)S(1)}, f32[128]{0:T(128)}, u32[]{:S(2)}) copy-start(f32[128]{0:T(128)} %param.26) | copy-start | bytes 1540
  275.7 33.9 %all-to-all-start.2 = ((bf16[128,16,224]{0,2,1:T(8,128)(2,1)}), bf16[128,16,224]{0,2,1:T(8,128)(2,1)}, u32[]{:S(2)}, u32[]{:S(2)}) async-start(bf16[128,16,224]{0,2,1:T(8,128)(2,1)} %bitcast.18), calls=%async_computation.2 | async-start | bytes 1835008 | tf_op jit(solution)/shard_map/all_to_all | solution.py:244
  303.7 2.9 copy-start.9
  306.6 41.9 %copy-start.1 = (bf16[5120,320]{0,1:T(8,128)(2,1)S(1)}, bf16[5120,320]{0,1:T(8,128)(2,1)}, u32[]{:S(2)}) copy-start(bf16[5120,320]{0,1:T(8,128)(2,1)} %param.19) | copy-start | bytes 9830404
Sparse Core Ops, SparseCore 0:
  56.3 54.9 all-gather.2
  127.9 131.4 all-reduce.1
  274.5 25.3 all-gather.4
where the time goes:
time: 356 us; the launch traced here: 355 us
  waiting for transfers between devices  219 us (62%)
  blocking collectives  35.3 us (10%)
  matrix products  34.1 us (10%)
  local copies, waits for them, and re-layouts  20.4 us (6%)
  other arithmetic  18.2 us (5%)
  between operations  15.5 us (4%)
  starting transfers between devices  12.9 us (4%)
    psum x1, waiting for transfers between devices, per_device(): summed = lax.psum(term, 'tp')  130 us
    all_gather x1, waiting for transfers between devices, per_device(): lax.all_gather(own_rows, 'tp', axis=0, tiled=True)  52.2 us
    all_to_all x1, blocking collectives, copy_for_each(): lax.all_to_all(jnp.broadcast_to(shard[None], (peers, *shard.shape)), axis...  35.3 us
    all_to_all x1, waiting for transfers between devices, per_device(): lax.all_to_all(outgoing, 'tp', split_axis=0, concat_axis=0, tiled=True)  20.6 us
    all_gather x1, waiting for transfers between devices, sent_together(): out, at, done = (lax.all_gather(both, axis, axis=dim, tiled=True), 0, [])  15.3 us
    dot_general x1, matrix products, per_device(): jnp.dot(hidden, merge_down, preferred_element_type=jnp.float32)  11.4 us
    all_to_all x1, starting transfers between devices, per_device(): lax.all_to_all(outgoing, 'tp', split_axis=0, concat_axis=0, tiled=True)  7.19 us
  transfers between devices with their start and end apart: 5, of which 4 were waited for; matrix products, arithmetic and copies ran while one was open for 5% of the time, Pallas kernels for 0%

commit v1 on v0

--- a/solution.py
+++ b/solution.py
@@ -112,6 +112,21 @@
     key_value_bias,
     o_weight,
 ):
+
+    def read_tasks(v0):
+        axis_len = jax.lax.axis_size("tp")
+
+        def settle_the_leaves(part_now, v_now):
+            if v_now >= axis_len:
+                return part_now
+            return settle_the_leaves(
+                part_now
+                + jax.lax.ppermute(part_now, "tp", [(w, w ^ v_now) for w in range(axis_len)]),
+                2 * v_now,
+            )
+
+        return settle_the_leaves(v0, 1)
+
     tp_count = lax.axis_size("tp")
     seq_index = lax.axis_index("seq")
     tensor_parallel_index = lax.axis_index("tp")
@@ -195,7 +210,7 @@
     )
     current = lax.dynamic_slice_in_dim(partial_sum, column_start, column_count, 1)
     term = lax.dynamic_update_slice_in_dim(partial_sum, current + text_rows, column_start, 1)
-    summed = lax.psum(term, "tp")
+    summed = read_tasks(term)
     residual = summed + image_weight[:, None] * merge_down_bias[None, :]
     scale_rows = lax.rsqrt(jnp.mean(residual * residual, axis=1) + EPS)
     normed_rows = (residual * scale_rows[:, None] * attn_gain[None, :]).astype(jnp.bfloat16)

time: 356 us -> 884 us (2.48)
  waiting for transfers between devices: 219 us -> 715 us
  other arithmetic: 18.2 us -> 41.9 us
  starting transfers between devices: 12.9 us -> 22.4 us
    ppermute x0 -> x4, waiting for transfers between devices: none -> 627 us  [settle_the_leaves(): jax.lax.ppermute(part_now, 'tp', [(w, w ^ v_now) for w in range(axis_len)])]
    psum x1 -> x0, waiting for transfers between devices: 130 us -> none  [per_device(): summed = lax.psum(term, 'tp')]
    add x0 -> x3, other arithmetic: none -> 21.3 us  [settle_the_leaves(): part_now + jax.lax.ppermute(part_now, 'tp', [(w, w ^ v_now) for w in rang...]
    ppermute x0 -> x4, starting transfers between devices: none -> 9.64 us  [settle_the_leaves(): jax.lax.ppermute(part_now, 'tp', [(w, w ^ v_now) for w in range(axis_len)])]
  transfers between devices with their start and end apart: 5 -> 8, of which waited for: 4 -> 7; matrix products, arithmetic and copies ran while one was open for 5% -> 2% of each run, Pallas kernels for 0% -> 0%
where the time goes in v1:
time: 884 us; the launch traced here: 883 us
  waiting for transfers between devices  715 us (81%)
  other arithmetic  41.9 us (5%)
  blocking collectives  35.3 us (4%)
  matrix products  34.1 us (4%)
  starting transfers between devices  22.4 us (3%)
  local copies, waits for them, and re-layouts  18.5 us (2%)
  between operations  15.8 us (2%)
    ppermute x4, waiting for transfers between devices, settle_the_leaves(): jax.lax.ppermute(part_now, 'tp', [(w, w ^ v_now) for w in range(axis_len)])  627 us
    all_gather x1, waiting for transfers between devices, per_device(): lax.all_gather(own_rows, 'tp', axis=0, tiled=True)  52.2 us
    all_to_all x1, blocking collectives, copy_for_each(): lax.all_to_all(jnp.broadcast_to(shard[None], (peers, *shard.shape)), axis...  35.3 us
    add x3, other arithmetic, settle_the_leaves(): part_now + jax.lax.ppermute(part_now, 'tp', [(w, w ^ v_now) for w in rang...  21.3 us
    all_to_all x1, waiting for transfers between devices, per_device(): lax.all_to_all(outgoing, 'tp', split_axis=0, concat_axis=0, tiled=True)  20.6 us
  transfers between devices with their start and end apart: 8, of which 7 were waited for; matrix products, arithmetic and copies ran while one was open for 2% of the time, Pallas kernels for 0%

profile of v1, /device:TPU:0, one launch (start us, length us, event | category | flops | bytes accessed | tf_op | source)
XLA Modules:
  0.0 883.0 jit_solution(17499374993265170354)
XLA Ops:
  13.9 2.3 fusion.13
  16.2 2.3 reshape.441
  19.1 2.4 convolution_convert_fusion
  21.5 2.2 reshape.442
  23.8 7.2 all-to-all-start
  31.2 20.6 %all-to-all-done = bf16[16,5,5120]{2,1,0:T(8,128)(2,1)} async-done(((bf16[16,5,5120]{2,1,0:T(8,128)(2,1)}), bf16[16,5,5120]{2,1,0:T(8,128)(2,1)}, u32[]{:S(2)}, u32[]{:S(2)}) %all-to-all-start) | async-done | bytes 819232 | tf_op jit(solution)/shard_map/all_to_all | solution.py:168
  51.8 2.2 reshape.443
  54.0 2.1 convolution_convert_fusion.1
  59.0 52.2 %all-gather.3.cloned.1.call-done = bf16[512,5120]{1,0:T(8,128)(2,1)} async-done(((bf16[32,5120]{1,0:T(8,128)(2,1)}), bf16[512,5120]{1,0:T(8,128)(2,1)}) %all-gather.3.cloned.1.call-update) | async-done | bytes 5242896 | tf_op jit(solution)/shard_map/all_gather | solution.py:182
  111.3 11.4 %fusion.41 = f32[512,3584]{1,0:T(8,128)} fusion(bf16[320,3584]{1,0:T(8,128)(2,1)} %param.21, bf16[512,5120]{1,0:T(8,128)(2,1)} %all-gather.3.cloned.1.call-done, bf16[5120,320]{0,1:T(8,128)(2,1)S(1)} %copy-done, f32[512]{0:T(512)S(1)} %get-tuple-element.28, f32[320]{0:T(512)S(1)} %copy-done.10), kind=kOutput, calls=%fused_computation.56 | convolution fusion | flops 2863104000 | bytes 18156800 | tf_op jit(solution)/shard_map/dot_general | solution.py:184
  124.2 3.5 dynamic_update_slice.3
  127.7 1.8 collective-permute-start
  129.5 158.1 %collective-permute-done = f32[512,3584]{1,0:T(8,128)} collective-permute-done((f32[512,3584]{1,0:T(8,128)}, f32[512,3584]{1,0:T(8,128)}, u32[]{:S(2)}, u32[]{:S(2)}) %collective-permute-start) | collective-permute-done | bytes 7340064 | tf_op jit(solution)/shard_map/ppermute | solution.py:124
  287.6 6.5 add.374
  294.1 3.5 collective-permute-start.1
  297.6 157.1 %collective-permute-done.1 = f32[512,3584]{1,0:T(8,128)} collective-permute-done((f32[512,3584]{1,0:T(8,128)S(1)}, f32[512,3584]{1,0:T(8,128)}, u32[]{:S(2)}, u32[]{:S(2)}) %collective-permute-start.1) | collective-permute-done | bytes 7340064 | tf_op jit(solution)/shard_map/ppermute | solution.py:124
  454.7 7.4 add.375
  463.5 156.7 %collective-permute-done.2 = f32[512,3584]{1,0:T(8,128)S(1)} collective-permute-done((f32[512,3584]{1,0:T(8,128)}, f32[512,3584]{1,0:T(8,128)S(1)}, u32[]{:S(2)}, u32[]{:S(2)}) %collective-permute-start.2) | collective-permute-done | bytes 7340064 | tf_op jit(solution)/shard_map/ppermute | solution.py:124
  620.2 7.4 add.376
  627.6 2.9 collective-permute-start.3
  631.5 155.0 %collective-permute-done.3 = f32[512,3584]{1,0:T(8,128)} collective-permute-done((f32[512,3584]{1,0:T(8,128)}, f32[512,3584]{1,0:T(8,128)}, u32[]{:S(2)}, u32[]{:S(2)}) %collective-permute-start.3) | collective-permute-done | bytes 7340064 | tf_op jit(solution)/shard_map/ppermute | solution.py:124
  786.5 6.5 multiply_reduce_fusion
  794.3 3.3 convolution_add_fusion.3
  797.7 2.6 fusion.17
  803.3 5.5 all-to-all-start.2
  808.9 3.4 convolution_add_fusion.1
  812.3 15.3 %all-gather.5.cloned.1.call-done = bf16[4096,256]{0,1:T(8,128)(2,1)} async-done(((bf16[512,256]{0,1:T(8,128)(2,1)}), bf16[4096,256]{0,1:T(8,128)(2,1)}) %all-gather.5.cloned.1.call-update) | async-done | bytes 2097168 | tf_op jit(solution)/shard_map/all_gather | solution.py:18
  827.6 3.8 fusion
  831.4 2.9 fusion.1
  834.3 3.0 fusion.21
  837.7 35.3 %all_to_all.26 = bf16[16,512,128]{2,1,0:T(8,128)(2,1)S(1)} all-to-all(bf16[16,512,128]{2,1,0:T(8,128)(2,1)S(1)} %broadcast_in_dim.60), channel_id=1, replica_groups=mesh['seq'=8,'tp'=16] {'tp'}, dimensions={0} | all-to-all | bytes 4194304 | tf_op jit(solution)/shard_map/all_to_all | solution.py:27
  873.0 2.1 add_convert_fusion
  (73 shorter events, 18.7 us)
Async XLA Ops:
  6.5 104.7 %copy-start = (bf16[5120,320]{0,1:T(8,128)(2,1)S(1)}, bf16[5120,320]{0,1:T(8,128)(2,1)}, u32[]{:S(2)}) copy-start(bf16[5120,320]{0,1:T(8,128)(2,1)} %param.19) | copy-start | bytes 9830404
  13.9 97.4 %copy-start.10 = (f32[320]{0:T(512)S(1)}, f32[320]{0:T(512)}, u32[]{:S(2)}) copy-start(f32[320]{0:T(512)} %param.20) | copy-start | bytes 3844
  23.8 28.1 %all-to-all-start = ((bf16[16,5,5120]{2,1,0:T(8,128)(2,1)}), bf16[16,5,5120]{2,1,0:T(8,128)(2,1)}, u32[]{:S(2)}, u32[]{:S(2)}) async-start(bf16[16,5,5120]{2,1,0:T(8,128)(2,1)} %reshape.442), calls=%async_computation | async-start | bytes 2621440 | tf_op jit(solution)/shard_map/all_to_all | solution.py:168
  31.0 80.3 %all-gather.3.cloned.1.call-start = ((), (), s32[]{:S(2)}) async-start(), calls=%async_computation.3 | async-start | bytes 5570560 | tf_op jit(solution)/shard_map/all_gather | solution.py:182
  56.1 771.4 %all-gather.5.cloned.1.call-start = ((), (), s32[]{:S(2)}) async-start(), calls=%async_computation.4 | async-start | bytes 2359296 | tf_op jit(solution)/shard_map/all_gather | solution.py:18
  127.7 159.9 %collective-permute-start = (f32[512,3584]{1,0:T(8,128)}, f32[512,3584]{1,0:T(8,128)}, u32[]{:S(2)}, u32[]{:S(2)}) collective-permute-start(f32[512,3584]{1,0:T(8,128)} %dynamic_update_slice.3), channel_id=1, source_target_pairs={{0,1},{1,0},{2,3},{3,2},{4,5},{5,4},{6,7},{7,6},{8,9},{9,8},{10,11... | collective-permute-start | bytes 22020104 | tf_op jit(solution)/shard_map/ppermute | solution.py:124
  294.1 160.6 %collective-permute-start.1 = (f32[512,3584]{1,0:T(8,128)S(1)}, f32[512,3584]{1,0:T(8,128)}, u32[]{:S(2)}, u32[]{:S(2)}) collective-permute-start(f32[512,3584]{1,0:T(8,128)S(1)} %add.374), channel_id=1, source_target_pairs={{0,2},{1,3},{2,0},{3,1},{4,6},{5,7},{6,4},{7,5},{8,10},{9,11},{10,... | collective-permute-start | bytes 22020104 | tf_op jit(solution)/shard_map/ppermute | solution.py:124
  462.1 324.4 %copy-start.7 = (f32[3584]{0:T(1024)S(1)}, f32[3584]{0:T(1024)}, u32[]{:S(2)}) copy-start(f32[3584]{0:T(1024)} %param.22) | copy-start | bytes 43012
  462.1 158.1 %collective-permute-start.2 = (f32[512,3584]{1,0:T(8,128)}, f32[512,3584]{1,0:T(8,128)S(1)}, u32[]{:S(2)}, u32[]{:S(2)}) collective-permute-start(f32[512,3584]{1,0:T(8,128)} %add.375), channel_id=1, source_target_pairs={{0,4},{1,5},{2,6},{3,7},{4,0},{5,1},{6,2},{7,3},{8,12},{9,13},{10,... | collective-permute-start | bytes 22020104 | tf_op jit(solution)/shard_map/ppermute | solution.py:124
  627.6 158.8 %collective-permute-start.3 = (f32[512,3584]{1,0:T(8,128)}, f32[512,3584]{1,0:T(8,128)}, u32[]{:S(2)}, u32[]{:S(2)}) collective-permute-start(f32[512,3584]{1,0:T(8,128)} %add.376), channel_id=1, source_target_pairs={{0,8},{1,9},{2,10},{3,11},{4,12},{5,13},{6,14},{7,15},{8,0},{9,1},... | collective-permute-start | bytes 22020104 | tf_op jit(solution)/shard_map/ppermute | solution.py:124
  631.5 161.5 %copy-start.6 = (f32[3584]{0:T(1024)S(1)}, f32[3584]{0:T(1024)}, u32[]{:S(2)}) copy-start(f32[3584]{0:T(1024)} %param.24) | copy-start | bytes 43012
  793.0 4.6 copy-start.3
  794.2 7.0 copy-start.2
  794.3 7.8 copy-start.4
  797.6 11.2 %copy-start.5 = (bf16[3584,128]{1,0:T(8,128)(2,1)S(1)}, bf16[3584,128]{1,0:T(8,128)(2,1)}, u32[]{:S(2)}) copy-start(bf16[3584,128]{1,0:T(8,128)(2,1)} %param.25) | copy-start | bytes 2752516
  797.6 11.2 %copy-start.8 = (f32[128]{0:T(128)S(1)}, f32[128]{0:T(128)}, u32[]{:S(2)}) copy-start(f32[128]{0:T(128)} %param.26) | copy-start | bytes 1540
  803.3 33.9 %all-to-all-start.2 = ((bf16[128,16,224]{0,2,1:T(8,128)(2,1)}), bf16[128,16,224]{0,2,1:T(8,128)(2,1)}, u32[]{:S(2)}, u32[]{:S(2)}) async-start(bf16[128,16,224]{0,2,1:T(8,128)(2,1)} %bitcast.18), calls=%async_computation.2 | async-start | bytes 1835008 | tf_op jit(solution)/shard_map/all_to_all | solution.py:259
  831.4 2.9 copy-start.9
  834.3 41.9 %copy-start.1 = (bf16[5120,320]{0,1:T(8,128)(2,1)S(1)}, bf16[5120,320]{0,1:T(8,128)(2,1)}, u32[]{:S(2)}) copy-start(bf16[5120,320]{0,1:T(8,128)(2,1)} %param.19) | copy-start | bytes 9830404
Sparse Core Ops, SparseCore 0:
  56.3 54.9 all-gather.2
  802.1 25.3 all-gather.4
